TPU v7x, 32 devices: a whole 2x2x4 slice. The times are simulated.
32 devices in a mesh: front: 4 (over y, core), row: 8 (over z, x).
Axes of the slice: x: 2, y: 2, z: 4, core: 2. Of those that a mesh axis runs over, the one named last changes fastest.
Arguments:
- rhs_diag: float32 [4, 32, 2048], P('front', None, 'row'), may hold values from -6 to 6
- rhs_off: float32 [4, 32, 12288], P('front', None, 'row'), may hold values from -6 to 6
- diag_factor: float32 [4, 2048, 2048], P('front', 'row'), may hold values from -0.125 to 0.125
- off_factor: float32 [4, 12288, 2048], P('front', 'row'), may hold values from -0.125 to 0.125
- diag_inverse: float32 [4, 4, 512, 512], P('front')
- pattern: int32 [4, 4, 96], P('front', None, 'row'), may hold values 0 or 1
- upd_vals: float32 [32, 4, 8, 4, 8, 128], P(None, 'front', 'row'), may hold values from -4 to 4
- upd_rows: int32 [4, 8, 4, 8, 128], P('front', 'row'), may hold values from 0 to 1791
Outputs:
- solved: float32 [4, 32, 2048], P('front', None, 'row')
- remainder: float32 [4, 32, 12288], P('front', None, 'row')
Inputs may be any that keep to these rules, and one draw needn't show every extreme that they name: `upd_rows`: relative rows of the receiving row block: below 256 a window row, else a row below the window; several entries may name one row.
All inputs are finite; a program needn't handle non-finite values. No bound on the sum of `pattern` on one device may be relied on, other than what follows from the above.
Results may differ from a plain program's by a relative error of at most 0.0001.
Values sent between devices are 32-bit elements; how exact they have to be, the bound alone decides.
A program may use at most 128 MiB of HBM per device.

v0:
```python
import jax
import jax.numpy as jnp
from jax import lax
from jax.sharding import PartitionSpec as P

W = 512
P_SIZE = 4
BR = 128


def local(rhs_diag, rhs_off, diag_factor, off_factor, diag_inverse, pattern, upd_vals, upd_rows):
    own_rows = diag_factor.shape[1]
    nrhs_count = upd_vals.shape[0]
    fronts_all = upd_vals.shape[3]
    groups_all = upd_vals.shape[4]
    slot_count = upd_vals.shape[5]
    flat_vals = upd_vals.reshape(nrhs_count, 1, fronts_all * groups_all, slot_count)
    arrived = lax.all_to_all(flat_vals, ("front", "row"), split_axis=2, concat_axis=1, tiled=True)
    received = arrived.reshape(nrhs_count, -1)
    targets = upd_rows.reshape(-1)
    combined = jnp.concatenate([rhs_diag[0], rhs_off[0]], axis=1)
    combined = combined.at[:, targets].add(received)
    upper = combined[:, :own_rows]
    lower = combined[:, own_rows:]
    diag_local = diag_factor[0]
    off_local = off_factor[0]
    inverse = diag_inverse[0]
    mask_rows = jnp.repeat(pattern[0].astype(jnp.float32), BR, axis=1)
    group = lax.axis_index("row")
    positions = group * own_rows + lax.iota(jnp.int32, own_rows)
    columns = lax.iota(jnp.int32, W)
    highest = lax.Precision.HIGHEST
    contract = (((1,), (1,)), ((), ()))
    pieces = []
    for panel in range(P_SIZE):
        picker = (
            (positions[:, None] // W == panel) & (positions[:, None] % W == columns[None, :])
        ).astype(jnp.float32)
        partial_rhs = jnp.dot(upper, picker, precision=highest, preferred_element_type=jnp.float32)
        panel_rhs = lax.psum(partial_rhs, "row")
        piece = lax.dot_general(
            panel_rhs,
            inverse[panel],
            contract,
            precision=highest,
            preferred_element_type=jnp.float32,
        )
        pieces.append(piece)
        upper = upper - lax.dot_general(
            piece,
            diag_local[:, panel * W : (panel + 1) * W],
            contract,
            precision=highest,
            preferred_element_type=jnp.float32,
        )
        term = lax.dot_general(
            piece,
            off_local[:, panel * W : (panel + 1) * W],
            contract,
            precision=highest,
            preferred_element_type=jnp.float32,
        )
        lower = lower - term * mask_rows[panel][None, :]
    solution = jnp.concatenate(pieces, axis=1)
    own_solution = lax.dynamic_slice_in_dim(solution, group * own_rows, own_rows, 1)
    return (own_solution[None], lower[None])


def solution(mesh):
    in_specs = (
        P("front", None, "row"),
        P("front", None, "row"),
        P("front", "row", None),
        P("front", "row", None),
        P("front", None, None, None),
        P("front", None, "row"),
        P(None, "front", "row", None, None, None),
        P("front", "row", None, None, None),
    )
    out_specs = (P("front", None, "row"), P("front", None, "row"))
    return jax.shard_map(local, mesh=mesh, in_specs=in_specs, out_specs=out_specs, check_vma=False)
```

profile of v0, /device:TPU:0, one launch (start us, length us, event | category | flops | bytes accessed | tf_op | source)
XLA Modules:
  0.0 367.9 jit_solution(12900171675111309321)
XLA Ops:
  7.2 2.1 copy.19
  9.3 7.3 %all-to-all-start = ((f32[32,1,32,128]{3,0,1,2:T(8,128)}), f32[32,1,32,128]{3,0,1,2:T(8,128)S(1)}, u32[]{:S(2)}, u32[]{:S(2)}) async-start(f32[32,1,32,128]{3,0,1,2:T(8,128)} %bitcast.4), calls=%async_computation | async-start | bytes 1048576 | tf_op jit(solution)/shard_map/all_to_all | solution.py:18
  17.9 0.9 pad_maximum_fusion
  22.3 10.5 %all-to-all-done = f32[32,1,32,128]{3,0,1,2:T(8,128)S(1)} async-done(((f32[32,1,32,128]{3,0,1,2:T(8,128)}), f32[32,1,32,128]{3,0,1,2:T(8,128)S(1)}, u32[]{:S(2)}, u32[]{:S(2)}) %all-to-all-start) | async-done | bytes 524320 | tf_op jit(solution)/shard_map/all_to_all | solution.py:18
  34.1 22.7 %scatter_fusion = f32[32,1792]{0,1:T(8,128)S(1)} fusion(f32[32,1792]{0,1:T(8,128)S(1)} %copy.21, s32[4096]{0:T(1024)S(1)} %bitcast.72, f32[4096,32]{1,0:T(8,128)S(1)} %copy.22), kind=kCustom, calls=%fused_computation | custom fusion | flops 131072 | bytes 1589248 | tf_op jit(solution)/shard_map/scatter-add | solution.py:22
  56.9 1.0 fusion.54
  58.1 67.0 %all-reduce.5.cloned.1.call-done = f32[32,512]{1,0:T(8,128)} async-done(((f32[32,512]{1,0:T(8,128)}), f32[32,512]{1,0:T(8,128)}) %all-reduce.5.cloned.1.call-update) | async-done | bytes 65552 | tf_op jit(solution)/shard_map/psum | solution.py:40
  125.1 2.3 fusion.41
  127.4 1.6 convolution_subtract_fusion.2
  129.0 1.0 fusion.56
  130.4 69.0 %all-reduce.7.cloned.1.call-done = f32[32,512]{1,0:T(8,128)} async-done(((f32[32,512]{1,0:T(8,128)}), f32[32,512]{1,0:T(8,128)}) %all-reduce.7.cloned.1.call-update) | async-done | bytes 65552 | tf_op jit(solution)/shard_map/psum | solution.py:40
  199.4 2.3 fusion.39
  201.7 1.6 convolution_subtract_fusion.1
  203.4 1.0 fusion.58
  204.6 4.8 %fusion.23 = f32[32,1536]{1,0:T(8,128)S(1)} fusion(f32[32,512]{1,0:T(8,128)S(1)} %fusion.39, f32[1536,2048]{1,0:T(8,128)} %bitcast.62, f32[1536]{0:T(1024)S(1)} %copy-done.3), kind=kOutput, calls=%fused_computation.14 | convolution fusion | flops 302039040 | bytes 3414016 | tf_op jit(solution)/shard_map/dot_general | solution.py:56
  209.4 64.3 %all-reduce.9.cloned.1.call-done = f32[32,512]{1,0:T(8,128)} async-done(((f32[32,512]{1,0:T(8,128)}), f32[32,512]{1,0:T(8,128)}) %all-reduce.9.cloned.1.call-update) | async-done | bytes 65552 | tf_op jit(solution)/shard_map/psum | solution.py:40
  273.7 2.3 fusion.37
  276.1 1.6 convolution_subtract_fusion
  277.7 1.0 fusion.60
  278.7 4.8 %fusion.26 = f32[32,1536]{1,0:T(8,128)S(1)} fusion(f32[32,512]{1,0:T(8,128)S(1)} %fusion.37, f32[1536,2048]{1,0:T(8,128)} %bitcast.63, f32[1536]{0:T(1024)S(1)} %copy-done.2), kind=kOutput, calls=%fused_computation.15 | convolution fusion | flops 302039040 | bytes 3414016 | tf_op jit(solution)/shard_map/dot_general | solution.py:56
  283.5 64.5 %all-reduce.11.cloned.1.call-done = f32[32,512]{1,0:T(8,128)} async-done(((f32[32,512]{1,0:T(8,128)}), f32[32,512]{1,0:T(8,128)}) %all-reduce.11.cloned.1.call-update) | async-done | bytes 65552 | tf_op jit(solution)/shard_map/psum | solution.py:40
  348.1 2.3 fusion.35
  350.4 4.8 %fusion.29 = f32[32,1536]{1,0:T(8,128)S(1)} fusion(f32[32,512]{1,0:T(8,128)S(1)} %fusion.35, f32[1536,2048]{1,0:T(8,128)} %bitcast.64, f32[1536]{0:T(1024)S(1)} %copy-done.1), kind=kOutput, calls=%fused_computation.16 | convolution fusion | flops 302039040 | bytes 3414016 | tf_op jit(solution)/shard_map/dot_general | solution.py:56
  355.8 5.5 %fusion.32 = f32[1,32,1536]{2,1,0:T(8,128)} fusion(f32[32,1536]{1,0:T(8,128)S(1)} %fusion.29, f32[32,1536]{1,0:T(8,128)S(1)} %fusion.26, f32[32,1536]{1,0:T(8,128)S(1)} %fusion.23, f32[32,1536]{1,0:T(8,128)S(1)} %copy.26, f32[32,512]{1,0:T(8,128)S(1)} %fusion.41, f32[1536,2048]{1,0:T(8,128)} %bitcast.65, f32[1536]{0:T(1024)S(1)} %copy-done), kind=kOutput, calls=%fused_computation.17 | convolution fusion | flops 302235648 | bytes 4200448 | tf_op jit(solution)/shard_map/dot_general | solution.py:56
  (43 shorter events, 7.4 us)
Async XLA Ops:
  9.3 23.6 %all-to-all-start = ((f32[32,1,32,128]{3,0,1,2:T(8,128)}), f32[32,1,32,128]{3,0,1,2:T(8,128)S(1)}, u32[]{:S(2)}, u32[]{:S(2)}) async-start(f32[32,1,32,128]{3,0,1,2:T(8,128)} %bitcast.4), calls=%async_computation | async-start | bytes 1048576 | tf_op jit(solution)/shard_map/all_to_all | solution.py:18
  16.6 108.5 %all-reduce.5.cloned.1.call-start = ((), (), s32[]{:S(2)}) async-start(), calls=%async_computation.1 | async-start | bytes 131072 | tf_op jit(solution)/shard_map/psum | solution.py:40
  34.1 22.8 %copy-start.4 = (s32[256]{0:T(256)S(1)}, s32[256]{0:T(256)}, u32[]{:S(2)}) copy-start(s32[256]{0:T(256)} %and_select_fusion) | copy-start | bytes 3076
  34.1 22.8 %copy-start.7 = (pred[256]{0:T(512)(128)(4,1)S(1)}, pred[256]{0:T(512)(128)(4,1)}, u32[]{:S(2)}) copy-start(pred[256]{0:T(512)(128)(4,1)} %broadcast_compare_fusion.2) | copy-start | bytes 772
  34.1 94.9 %copy-start.6 = (pred[256]{0:T(512)(128)(4,1)S(1)}, pred[256]{0:T(512)(128)(4,1)}, u32[]{:S(2)}) copy-start(pred[256]{0:T(512)(128)(4,1)} %broadcast_compare_fusion.4) | copy-start | bytes 772
  56.9 146.5 %copy-start.5 = (s32[256]{0:T(256)S(1)}, s32[256]{0:T(256)}, u32[]{:S(2)}) copy-start(s32[256]{0:T(256)} %and_select_fusion) | copy-start | bytes 3076
  56.9 147.7 %copy-start.3 = (f32[1536]{0:T(1024)S(1)}, f32[1536]{0:T(1024)}, u32[]{:S(2)}) copy-start(f32[1536]{0:T(1024)} %get-tuple-element.8) | copy-start | bytes 18436
  57.9 141.5 %all-reduce.7.cloned.1.call-start = ((), (), s32[]{:S(2)}) async-start(), calls=%async_computation.2 | async-start | bytes 131072 | tf_op jit(solution)/shard_map/psum | solution.py:40
  130.1 143.7 %all-reduce.9.cloned.1.call-start = ((), (), s32[]{:S(2)}) async-start(), calls=%async_computation.3 | async-start | bytes 131072 | tf_op jit(solution)/shard_map/psum | solution.py:40
  130.2 148.5 %copy-start.2 = (f32[1536]{0:T(1024)S(1)}, f32[1536]{0:T(1024)}, u32[]{:S(2)}) copy-start(f32[1536]{0:T(1024)} %get-tuple-element.7) | copy-start | bytes 18436
  204.4 143.7 %all-reduce.11.cloned.1.call-start = ((), (), s32[]{:S(2)}) async-start(), calls=%async_computation.4 | async-start | bytes 131072 | tf_op jit(solution)/shard_map/psum | solution.py:40
  209.4 140.9 %copy-start.1 = (f32[1536]{0:T(1024)S(1)}, f32[1536]{0:T(1024)}, u32[]{:S(2)}) copy-start(f32[1536]{0:T(1024)} %get-tuple-element.6) | copy-start | bytes 18436
  278.7 77.2 %copy-start = (f32[1536]{0:T(1024)S(1)}, f32[1536]{0:T(1024)}, u32[]{:S(2)}) copy-start(f32[1536]{0:T(1024)} %get-tuple-element.9) | copy-start | bytes 18436
Sparse Core Ops, SparseCore 0:
  58.0 66.9 all-reduce.4
  130.2 69.1 all-reduce.6
  204.5 69.1 all-reduce.8
  278.8 69.1 all-reduce.10
where the time goes:
time: 369 us; the launch traced here: 368 us
  waiting for transfers between devices  275 us (75%)
  matrix products  37.9 us (10%)
  other arithmetic  27.4 us (7%)
  between operations  14 us (4%)
  starting transfers between devices  7.67 us (2%)
  local copies, waits for them, and re-layouts  5.4 us (1%)
    psum x4, waiting for transfers between devices, local(): panel_rhs = lax.psum(partial_rhs, 'row')  265 us
    scatter-add x1, other arithmetic, local(): combined = combined.at[:, targets].add(received)  22.7 us
    dot_general x4, matrix products, local(): lax.dot_general(piece, off_local[:, panel * W:(panel + 1) * W], contract,...  19.9 us
    all_to_all x1, waiting for transfers between devices, local(): lax.all_to_all(flat_vals, ('front', 'row'), split_axis=2, concat_axis=1,...  10.5 us
    dot_general x4, matrix products, local(): lax.dot_general(panel_rhs, inverse[panel], contract, precision=highest, p...  9.18 us
  transfers between devices with their start and end apart: 5, of which 5 were waited for; matrix products, arithmetic and copies ran while one was open for 4% of the time, Pallas kernels for 0%

commit v1 on v0

--- a/solution.py
+++ b/solution.py
@@ -6,6 +6,15 @@
 W = 512
 P_SIZE = 4
 BR = 128
+
+
+def added_up(x, mesh_axis):
+    count = lax.axis_size(mesh_axis)
+    total, hop = (x, 1)
+    while hop < count:
+        total = total + lax.ppermute(total, mesh_axis, [(i, i ^ hop) for i in range(count)])
+        hop = 2 * hop
+    return total
 
 
 def local(rhs_diag, rhs_off, diag_factor, off_factor, diag_inverse, pattern, upd_vals, upd_rows):
@@ -37,7 +46,7 @@
             (positions[:, None] // W == panel) & (positions[:, None] % W == columns[None, :])
         ).astype(jnp.float32)
         partial_rhs = jnp.dot(upper, picker, precision=highest, preferred_element_type=jnp.float32)
-        panel_rhs = lax.psum(partial_rhs, "row")
+        panel_rhs = added_up(partial_rhs, "row")
         piece = lax.dot_general(
             panel_rhs,
             inverse[panel],

time: 369 us -> 137 us (0.37)
  waiting for transfers between devices: 275 us -> 56.1 us
  between operations: 14 us -> 0.94 us
  starting transfers between devices: 7.67 us -> 12.8 us
    psum x4 -> x0, waiting for transfers between devices: 265 us -> none  [local(): panel_rhs = lax.psum(partial_rhs, 'row')]
    ppermute x0 -> x12, waiting for transfers between devices: none -> 43 us  [added_up(): lax.ppermute(total, mesh_axis, [(i, i ^ hop) for i in range(count)])]
    ppermute x0 -> x12, starting transfers between devices: none -> 5.45 us  [added_up(): lax.ppermute(total, mesh_axis, [(i, i ^ hop) for i in range(count)])]
  transfers between devices with their start and end apart: 5 -> 13, of which waited for: 5 -> 11; matrix products, arithmetic and copies ran while one was open for 4% -> 10% of each run, Pallas kernels for 0% -> 0%
where the time goes in v1:
time: 137 us; the launch traced here: 136 us
  waiting for transfers between devices  56.1 us (41%)
  matrix products  34.8 us (25%)
  other arithmetic  27.1 us (20%)
  starting transfers between devices  12.8 us (9%)
  local copies, waits for them, and re-layouts  4.24 us (3%)
    ppermute x12, waiting for transfers between devices, added_up(): lax.ppermute(total, mesh_axis, [(i, i ^ hop) for i in range(count)])  43 us
    scatter-add x1, other arithmetic, local(): combined = combined.at[:, targets].add(received)  22.9 us
    dot_general x4, matrix products, local(): lax.dot_general(piece, off_local[:, panel * W:(panel + 1) * W], contract,...  20.1 us
    all_to_all x1, waiting for transfers between devices, local(): lax.all_to_all(flat_vals, ('front', 'row'), split_axis=2, concat_axis=1,...  13.1 us
    dot_general x4, matrix products, local(): lax.dot_general(panel_rhs, inverse[panel], contract, precision=highest, p...  9.03 us
    all_to_all x1, starting transfers between devices, local(): lax.all_to_all(flat_vals, ('front', 'row'), split_axis=2, concat_axis=1,...  7.33 us
    ppermute x12, starting transfers between devices, added_up(): lax.ppermute(total, mesh_axis, [(i, i ^ hop) for i in range(count)])  5.45 us
    dot_general x4, matrix products, local(): jnp.dot(upper, picker, precision=highest, preferred_element_type=jnp.floa...  2.97 us
  transfers between devices with their start and end apart: 13, of which 11 were waited for; matrix products, arithmetic and copies ran while one was open for 10% of the time, Pallas kernels for 0%

profile of v1, /device:TPU:0, one launch (start us, length us, event | category | flops | bytes accessed | tf_op | source)
XLA Modules:
  0.0 136.1 jit_solution(16465550207153580345)
XLA Ops:
  0.6 2.1 %copy.19 = f32[32,1,1,4,8,128]{5,0,4,3,2,1:T(8,128)} copy(f32[32,1,1,4,8,128]{5,4,3,2,1,0:T(8,128)} %param.14) | data formatting | bytes 1048576 | tf_op args[6]
  2.8 7.3 %all-to-all-start = ((f32[32,1,32,128]{3,0,1,2:T(8,128)}), f32[32,1,32,128]{3,0,1,2:T(8,128)S(1)}, u32[]{:S(2)}, u32[]{:S(2)}) async-start(f32[32,1,32,128]{3,0,1,2:T(8,128)} %bitcast.4), calls=%async_computation | async-start | bytes 1048576 | tf_op jit(solution)/shard_map/all_to_all | solution.py:27
  13.2 13.1 %all-to-all-done = f32[32,1,32,128]{3,0,1,2:T(8,128)S(1)} async-done(((f32[32,1,32,128]{3,0,1,2:T(8,128)}), f32[32,1,32,128]{3,0,1,2:T(8,128)S(1)}, u32[]{:S(2)}, u32[]{:S(2)}) %all-to-all-start) | async-done | bytes 524320 | tf_op jit(solution)/shard_map/all_to_all | solution.py:27
  27.6 22.9 %scatter_fusion = f32[32,1792]{0,1:T(8,128)S(1)} fusion(f32[32,1792]{0,1:T(8,128)S(1)} %copy.21, s32[4096]{0:T(1024)S(1)} %bitcast.68, f32[4096,32]{1,0:T(8,128)S(1)} %copy.22), kind=kCustom, calls=%fused_computation | custom fusion | flops 131072 | bytes 1589248 | tf_op jit(solution)/shard_map/scatter-add | solution.py:31
  52.7 3.3 %collective-permute-done = f32[32,512]{1,0:T(8,128)S(1)} collective-permute-done((f32[32,512]{1,0:T(8,128)S(1)}, f32[32,512]{1,0:T(8,128)S(1)}, u32[]{:S(2)}, u32[]{:S(2)}) %collective-permute-start) | collective-permute-done | bytes 65568 | tf_op jit(solution)/shard_map/ppermute | solution.py:15
  56.9 3.5 %collective-permute-done.1 = f32[32,512]{1,0:T(8,128)S(1)} collective-permute-done((f32[32,512]{1,0:T(8,128)S(1)}, f32[32,512]{1,0:T(8,128)S(1)}, u32[]{:S(2)}, u32[]{:S(2)}) %collective-permute-start.1) | collective-permute-done | bytes 65568 | tf_op jit(solution)/shard_map/ppermute | solution.py:15
  60.6 5.8 %collective-permute-done.2 = f32[32,512]{1,0:T(8,128)S(1)} collective-permute-done((f32[32,512]{1,0:T(8,128)S(1)}, f32[32,512]{1,0:T(8,128)S(1)}, u32[]{:S(2)}, u32[]{:S(2)}) %collective-permute-start.2) | collective-permute-done | bytes 65568 | tf_op jit(solution)/shard_map/ppermute | solution.py:15
  66.3 2.3 %fusion.41 = f32[32,512]{1,0:T(8,128)S(1)} fusion(f32[1,4,512,512]{3,2,1,0:T(8,128)} %param.12, f32[32,512]{1,0:T(8,128)S(1)} %add.114, f32[32,512]{1,0:T(8,128)S(1)} %collective-permute-done.2), kind=kOutput, calls=%fused_computation.27 | convolution fusion | flops 100679680 | bytes 1245184 | tf_op jit(solution)/shard_map/dot_general | solution.py:50
  68.6 1.6 %convolution_subtract_fusion.2 = f32[32,256]{1,0:T(8,128)S(1)} fusion(f32[32,256]{1,0:T(8,128)S(1)} %copy.25, f32[32,512]{1,0:T(8,128)S(1)} %fusion.41, f32[256,2048]{1,0:T(8,128)} %bitcast.64), kind=kOutput, calls=%fused_computation.20 | convolution fusion | flops 50339840 | bytes 655360 | tf_op jit(solution)/shard_map/dot_general | solution.py:58
  72.4 3.2 %collective-permute-done.3 = f32[32,512]{1,0:T(8,128)S(1)} collective-permute-done((f32[32,512]{1,0:T(8,128)S(1)}, f32[32,512]{1,0:T(8,128)S(1)}, u32[]{:S(2)}, u32[]{:S(2)}) %collective-permute-start.3) | collective-permute-done | bytes 65568 | tf_op jit(solution)/shard_map/ppermute | solution.py:15
  76.2 3.7 %collective-permute-done.4 = f32[32,512]{1,0:T(8,128)S(1)} collective-permute-done((f32[32,512]{1,0:T(8,128)S(1)}, f32[32,512]{1,0:T(8,128)S(1)}, u32[]{:S(2)}, u32[]{:S(2)}) %collective-permute-start.4) | collective-permute-done | bytes 65568 | tf_op jit(solution)/shard_map/ppermute | solution.py:15
  80.0 5.8 %collective-permute-done.5 = f32[32,512]{1,0:T(8,128)S(1)} collective-permute-done((f32[32,512]{1,0:T(8,128)S(1)}, f32[32,512]{1,0:T(8,128)S(1)}, u32[]{:S(2)}, u32[]{:S(2)}) %collective-permute-start.5) | collective-permute-done | bytes 65568 | tf_op jit(solution)/shard_map/ppermute | solution.py:15
  85.9 2.3 %fusion.39 = f32[32,512]{1,0:T(8,128)S(1)} fusion(f32[1,4,512,512]{3,2,1,0:T(8,128)} %param.12, f32[32,512]{1,0:T(8,128)S(1)} %add.117, f32[32,512]{1,0:T(8,128)S(1)} %collective-permute-done.5), kind=kOutput, calls=%fused_computation.25 | convolution fusion | flops 100679680 | bytes 1245184 | tf_op jit(solution)/shard_map/dot_general | solution.py:50
  89.4 4.1 %collective-permute-done.6 = f32[32,512]{1,0:T(8,128)S(1)} collective-permute-done((f32[32,512]{1,0:T(8,128)S(1)}, f32[32,512]{1,0:T(8,128)S(1)}, u32[]{:S(2)}, u32[]{:S(2)}) %collective-permute-start.6) | collective-permute-done | bytes 65568 | tf_op jit(solution)/shard_map/ppermute | solution.py:15
  93.6 4.2 %collective-permute-done.7 = f32[32,512]{1,0:T(8,128)S(1)} collective-permute-done((f32[32,512]{1,0:T(8,128)S(1)}, f32[32,512]{1,0:T(8,128)S(1)}, u32[]{:S(2)}, u32[]{:S(2)}) %collective-permute-start.7) | collective-permute-done | bytes 65568 | tf_op jit(solution)/shard_map/ppermute | solution.py:15
  97.9 5.6 %collective-permute-done.8 = f32[32,512]{1,0:T(8,128)S(1)} collective-permute-done((f32[32,512]{1,0:T(8,128)S(1)}, f32[32,512]{1,0:T(8,128)S(1)}, u32[]{:S(2)}, u32[]{:S(2)}) %collective-permute-start.8) | collective-permute-done | bytes 65568 | tf_op jit(solution)/shard_map/ppermute | solution.py:15
  103.5 2.3 %fusion.37 = f32[32,512]{1,0:T(8,128)S(1)} fusion(f32[1,4,512,512]{3,2,1,0:T(8,128)} %param.12, f32[32,512]{1,0:T(8,128)S(1)} %add.120, f32[32,512]{1,0:T(8,128)S(1)} %collective-permute-done.8), kind=kOutput, calls=%fused_computation.23 | convolution fusion | flops 100679680 | bytes 1245184 | tf_op jit(solution)/shard_map/dot_general | solution.py:50
  107.1 3.9 %collective-permute-done.9 = f32[32,512]{1,0:T(8,128)S(1)} collective-permute-done((f32[32,512]{1,0:T(8,128)S(1)}, f32[32,512]{1,0:T(8,128)S(1)}, u32[]{:S(2)}, u32[]{:S(2)}) %collective-permute-start.9) | collective-permute-done | bytes 65568 | tf_op jit(solution)/shard_map/ppermute | solution.py:15
  111.2 4.8 %fusion.23 = f32[32,1536]{1,0:T(8,128)S(1)} fusion(f32[32,512]{1,0:T(8,128)S(1)} %fusion.39, f32[1536,2048]{1,0:T(8,128)} %bitcast.58, f32[1536]{0:T(1024)S(1)} %broadcast_bitcast_fusion.2), kind=kOutput, calls=%fused_computation.14 | convolution fusion | flops 302039040 | bytes 3414016 | tf_op jit(solution)/shard_map/dot_general | solution.py:65
  116.0 1.8 %collective-permute-start.11 = (f32[32,512]{1,0:T(8,128)S(1)}, f32[32,512]{1,0:T(8,128)S(1)}, u32[]{:S(2)}, u32[]{:S(2)}) collective-permute-start(f32[32,512]{1,0:T(8,128)S(1)} %add.123), channel_id=1, source_target_pairs={{0,4},{1,5},{2,6},{3,7},{4,0},{5,1},{6,2},{7,3},{8,12},{9,13},{10,... | collective-permute-start | bytes 196616 | tf_op jit(solution)/shard_map/ppermute | solution.py:15
  117.8 4.8 %fusion.26 = f32[32,1536]{1,0:T(8,128)S(1)} fusion(f32[32,512]{1,0:T(8,128)S(1)} %fusion.37, f32[1536,2048]{1,0:T(8,128)} %bitcast.59, f32[1536]{0:T(1024)S(1)} %get-tuple-element.7), kind=kOutput, calls=%fused_computation.15 | convolution fusion | flops 302039040 | bytes 3414016 | tf_op jit(solution)/shard_map/dot_general | solution.py:65
  122.6 2.3 %fusion.35 = f32[32,512]{1,0:T(8,128)S(1)} fusion(f32[1,4,512,512]{3,2,1,0:T(8,128)} %param.12, f32[32,512]{1,0:T(8,128)S(1)} %add.123, f32[32,512]{1,0:T(8,128)S(1)} %collective-permute-done.11), kind=kOutput, calls=%fused_computation.21 | convolution fusion | flops 100679680 | bytes 1245184 | tf_op jit(solution)/shard_map/dot_general | solution.py:50
  124.9 5.0 %fusion.29 = f32[32,1536]{1,0:T(8,128)S(1)} fusion(f32[32,512]{1,0:T(8,128)S(1)} %fusion.35, f32[1536,2048]{1,0:T(8,128)} %bitcast.60, f32[1536]{0:T(1024)S(1)} %get-tuple-element.6), kind=kOutput, calls=%fused_computation.16 | convolution fusion | flops 302039040 | bytes 3414016 | tf_op jit(solution)/shard_map/dot_general | solution.py:65
  130.6 5.5 %fusion.32 = f32[1,32,1536]{2,1,0:T(8,128)} fusion(f32[32,1536]{1,0:T(8,128)S(1)} %fusion.29, f32[32,1536]{1,0:T(8,128)S(1)} %fusion.26, f32[32,1536]{1,0:T(8,128)S(1)} %fusion.23, f32[32,1536]{1,0:T(8,128)S(1)} %copy.26, f32[32,512]{1,0:T(8,128)S(1)} %fusion.41, f32[1536,2048]{1,0:T(8,128)} %bitcast.61, f32[1536]{0:T(1024)S(1)} %broadcast_bitcast_fusion.3), kind=kOutput, calls=%fused_computation.17 | convolution fusion | flops 302235648 | bytes 4200448 | tf_op jit(solution)/shard_map/dot_general | solution.py:65
  (52 shorter events, 14.1 us)
Async XLA Ops:
  2.8 23.6 %all-to-all-start = ((f32[32,1,32,128]{3,0,1,2:T(8,128)}), f32[32,1,32,128]{3,0,1,2:T(8,128)S(1)}, u32[]{:S(2)}, u32[]{:S(2)}) async-start(f32[32,1,32,128]{3,0,1,2:T(8,128)} %bitcast.4), calls=%async_computation | async-start | bytes 1048576 | tf_op jit(solution)/shard_map/all_to_all | solution.py:27
  50.5 37.7 %copy-start = (f32[1,256,2048]{2,1,0:T(8,128)S(1)}, f32[1,256,2048]{2,1,0:T(8,128)}, u32[]{:S(2)}) copy-start(f32[1,256,2048]{2,1,0:T(8,128)} %param.10) | copy-start | bytes 6291460
  50.5 38.2 %copy-start.1 = (s32[256]{0:T(256)S(1)}, s32[256]{0:T(256)}, u32[]{:S(2)}) copy-start(s32[256]{0:T(256)} %and_select_fusion) | copy-start | bytes 3076
  51.7 4.3 %collective-permute-start = (f32[32,512]{1,0:T(8,128)S(1)}, f32[32,512]{1,0:T(8,128)S(1)}, u32[]{:S(2)}, u32[]{:S(2)}) collective-permute-start(f32[32,512]{1,0:T(8,128)S(1)} %fusion.54), channel_id=1, source_target_pairs={{0,1},{1,0},{2,3},{3,2},{4,5},{5,4},{6,7},{7,6},{8,9},{9,8},{10,11... | collective-permute-start | bytes 196616 | tf_op jit(solution)/shard_map/ppermute | solution.py:15
  56.0 4.3 %collective-permute-start.1 = (f32[32,512]{1,0:T(8,128)S(1)}, f32[32,512]{1,0:T(8,128)S(1)}, u32[]{:S(2)}, u32[]{:S(2)}) collective-permute-start(f32[32,512]{1,0:T(8,128)S(1)} %add.113), channel_id=1, source_target_pairs={{0,2},{1,3},{2,0},{3,1},{4,6},{5,7},{6,4},{7,5},{8,10},{9,11},{10,... | collective-permute-start | bytes 196616 | tf_op jit(solution)/shard_map/ppermute | solution.py:15
  60.4 5.9 %collective-permute-start.2 = (f32[32,512]{1,0:T(8,128)S(1)}, f32[32,512]{1,0:T(8,128)S(1)}, u32[]{:S(2)}, u32[]{:S(2)}) collective-permute-start(f32[32,512]{1,0:T(8,128)S(1)} %add.114), channel_id=1, source_target_pairs={{0,4},{1,5},{2,6},{3,7},{4,0},{5,1},{6,2},{7,3},{8,12},{9,13},{10,... | collective-permute-start | bytes 196616 | tf_op jit(solution)/shard_map/ppermute | solution.py:15
  71.3 4.3 %collective-permute-start.3 = (f32[32,512]{1,0:T(8,128)S(1)}, f32[32,512]{1,0:T(8,128)S(1)}, u32[]{:S(2)}, u32[]{:S(2)}) collective-permute-start(f32[32,512]{1,0:T(8,128)S(1)} %fusion.56), channel_id=1, source_target_pairs={{0,1},{1,0},{2,3},{3,2},{4,5},{5,4},{6,7},{7,6},{8,9},{9,8},{10,11... | collective-permute-start | bytes 196616 | tf_op jit(solution)/shard_map/ppermute | solution.py:15
  75.6 4.3 %collective-permute-start.4 = (f32[32,512]{1,0:T(8,128)S(1)}, f32[32,512]{1,0:T(8,128)S(1)}, u32[]{:S(2)}, u32[]{:S(2)}) collective-permute-start(f32[32,512]{1,0:T(8,128)S(1)} %add.116), channel_id=1, source_target_pairs={{0,2},{1,3},{2,0},{3,1},{4,6},{5,7},{6,4},{7,5},{8,10},{9,11},{10,... | collective-permute-start | bytes 196616 | tf_op jit(solution)/shard_map/ppermute | solution.py:15
  80.0 5.9 %collective-permute-start.5 = (f32[32,512]{1,0:T(8,128)S(1)}, f32[32,512]{1,0:T(8,128)S(1)}, u32[]{:S(2)}, u32[]{:S(2)}) collective-permute-start(f32[32,512]{1,0:T(8,128)S(1)} %add.117), channel_id=1, source_target_pairs={{0,4},{1,5},{2,6},{3,7},{4,0},{5,1},{6,2},{7,3},{8,12},{9,13},{10,... | collective-permute-start | bytes 196616 | tf_op jit(solution)/shard_map/ppermute | solution.py:15
  89.1 4.3 %collective-permute-start.6 = (f32[32,512]{1,0:T(8,128)S(1)}, f32[32,512]{1,0:T(8,128)S(1)}, u32[]{:S(2)}, u32[]{:S(2)}) collective-permute-start(f32[32,512]{1,0:T(8,128)S(1)} %fusion.58), channel_id=1, source_target_pairs={{0,1},{1,0},{2,3},{3,2},{4,5},{5,4},{6,7},{7,6},{8,9},{9,8},{10,11... | collective-permute-start | bytes 196616 | tf_op jit(solution)/shard_map/ppermute | solution.py:15
  93.5 4.3 %collective-permute-start.7 = (f32[32,512]{1,0:T(8,128)S(1)}, f32[32,512]{1,0:T(8,128)S(1)}, u32[]{:S(2)}, u32[]{:S(2)}) collective-permute-start(f32[32,512]{1,0:T(8,128)S(1)} %add.119), channel_id=1, source_target_pairs={{0,2},{1,3},{2,0},{3,1},{4,6},{5,7},{6,4},{7,5},{8,10},{9,11},{10,... | collective-permute-start | bytes 196616 | tf_op jit(solution)/shard_map/ppermute | solution.py:15
  97.8 5.7 %collective-permute-start.8 = (f32[32,512]{1,0:T(8,128)S(1)}, f32[32,512]{1,0:T(8,128)S(1)}, u32[]{:S(2)}, u32[]{:S(2)}) collective-permute-start(f32[32,512]{1,0:T(8,128)S(1)} %add.120), channel_id=1, source_target_pairs={{0,4},{1,5},{2,6},{3,7},{4,0},{5,1},{6,2},{7,3},{8,12},{9,13},{10,... | collective-permute-start | bytes 196616 | tf_op jit(solution)/shard_map/ppermute | solution.py:15
  106.7 4.3 %collective-permute-start.9 = (f32[32,512]{1,0:T(8,128)S(1)}, f32[32,512]{1,0:T(8,128)S(1)}, u32[]{:S(2)}, u32[]{:S(2)}) collective-permute-start(f32[32,512]{1,0:T(8,128)S(1)} %fusion.60), channel_id=1, source_target_pairs={{0,1},{1,0},{2,3},{3,2},{4,5},{5,4},{6,7},{7,6},{8,9},{9,8},{10,11... | collective-permute-start | bytes 196616 | tf_op jit(solution)/shard_map/ppermute | solution.py:15
  111.0 5.0 %collective-permute-start.10 = (f32[32,512]{1,0:T(8,128)S(1)}, f32[32,512]{1,0:T(8,128)S(1)}, u32[]{:S(2)}, u32[]{:S(2)}) collective-permute-start(f32[32,512]{1,0:T(8,128)S(1)} %add.122), channel_id=1, source_target_pairs={{0,2},{1,3},{2,0},{3,1},{4,6},{5,7},{6,4},{7,5},{8,10},{9,11},{10,... | collective-permute-start | bytes 196616 | tf_op jit(solution)/shard_map/ppermute | solution.py:15
  116.0 6.6 %collective-permute-start.11 = (f32[32,512]{1,0:T(8,128)S(1)}, f32[32,512]{1,0:T(8,128)S(1)}, u32[]{:S(2)}, u32[]{:S(2)}) collective-permute-start(f32[32,512]{1,0:T(8,128)S(1)} %add.123), channel_id=1, source_target_pairs={{0,4},{1,5},{2,6},{3,7},{4,0},{5,1},{6,2},{7,3},{8,12},{9,13},{10,... | collective-permute-start | bytes 196616 | tf_op jit(solution)/shard_map/ppermute | solution.py:15
